TPU v7x, 32 devices: a whole 2x2x4 slice. The times are simulated.
32 devices in a mesh: row: 8 (over y, x, core), col: 4 (over z).
Axes of the slice: x: 2, y: 2, z: 4, core: 2. Of those that a mesh axis runs over, the one named last changes fastest.
Arguments:
- tokens: bfloat16 [65536, 1024], P('row', 'col'), may hold values from -6 to 6
- up_weight: bfloat16 [1024, 4096], P('row', 'col'), may hold values from -0.1875 to 0.1875
- hidden_grad: bfloat16 [65536, 4096], P('row', 'col'), may hold values from -6 to 6
Outputs:
- hidden: bfloat16 [65536, 4096], P('row', 'col')
- input_grad: bfloat16 [65536, 1024], P('row', 'col')
All inputs are finite; a program needn't handle non-finite values.
Results may differ from a plain program's by a relative error of at most 0.017.
Values may be sent and summed in bfloat16 or wider, within the bound.
No kernel may reach another device: no remote copies, remote signals or barrier semaphores. Data moves between devices by JAX's collectives and lax.ppermute only.
A program may use at most 128 MiB of HBM per device.

v0:
```python
import jax
import jax.numpy as jnp
from jax import lax
from jax.sharding import PartitionSpec as P

gelu_c = 0.7978845608028654
gelu_a = 0.044715


def gelu_value(v):
    inner = gelu_c * (v + gelu_a * v * v * v)
    return 0.5 * v * (1.0 + jnp.tanh(inner))


def gelu_slope(v):
    inner = gelu_c * (v + gelu_a * v * v * v)
    tval = jnp.tanh(inner)
    return 0.5 * (1.0 + tval) + 0.5 * v * (1.0 - tval * tval) * gelu_c * (
        1.0 + 3.0 * gelu_a * v * v
    )


def per_device(tokens, up_weight, hidden_grad):
    column_panel = lax.all_gather(up_weight, "row", axis=0, tiled=True)
    token_rows = lax.all_gather(tokens, "col", axis=1, tiled=True)
    preact = jnp.dot(token_rows, column_panel, preferred_element_type=jnp.float32)
    hidden = gelu_value(preact).astype(jnp.bfloat16)
    pre_grad = (hidden_grad.astype(jnp.float32) * gelu_slope(preact)).astype(jnp.bfloat16)
    summed = lax.psum_scatter(
        lax.dot_general(
            column_panel, pre_grad, (((1,), (1,)), ((), ())), preferred_element_type=jnp.float32
        ).astype(jnp.bfloat16),
        "col",
        scatter_dimension=0,
        tiled=True,
    ).astype(jnp.float32)
    input_grad = jnp.transpose(summed).astype(jnp.bfloat16)
    return (hidden, input_grad)


def solution(mesh):
    in_specs = (P("row", "col"), P("row", "col"), P("row", "col"))
    out_specs = (P("row", "col"), P("row", "col"))
    return jax.shard_map(
        per_device, mesh=mesh, in_specs=in_specs, out_specs=out_specs, check_vma=False
    )
```

profile of v0, /device:TPU:0, one launch (start us, length us, event | category | flops | bytes accessed | tf_op | source)
XLA Modules:
  0.0 688.1 jit_solution(10581565400900481184)
XLA Ops:
  7.2 0.0 all-gather.5.cloned.1.call-start
  7.2 0.7 all-gather.5.cloned.1.call-update
  7.9 0.0 all-gather.3.cloned.1.call-start
  7.9 0.7 all-gather.3.cloned.1.call-update
  8.6 0.0 reduce-scatter.2.cloned.1.call-start
  8.7 31.7 %all-gather.5.cloned.1.call-done = bf16[1024,1024]{1,0:T(8,128)(2,1)} async-done(((bf16[128,1024]{1,0:T(8,128)(2,1)}), bf16[1024,1024]{1,0:T(8,128)(2,1)}) %all-gather.5.cloned.1.call-update) | async-done | bytes 2097168 | tf_op jit(solution)/shard_map/all_gather | solution.py:24
  40.4 0.0 copy-start
  40.4 287.8 %all-gather.3.cloned.1.call-done = bf16[8192,1024]{1,0:T(8,128)(2,1)} async-done(((bf16[8192,256]{1,0:T(8,128)(2,1)}), bf16[8192,1024]{1,0:T(8,128)(2,1)}) %all-gather.3.cloned.1.call-update) | async-done | bytes 16777232 | tf_op jit(solution)/shard_map/all_gather | solution.py:25
  328.2 34.3 %multiply_convert_fusion = (bf16[8192,1024]{1,0:T(8,128)(2,1)}, f32[8192,1024]{1,0:T(8,128)}) fusion(bf16[8192,1024]{1,0:T(8,128)(2,1)} %all-gather.3.cloned.1.call-done, bf16[1024,1024]{1,0:T(8,128)(2,1)} %all-gather.5.cloned.1.call-done), kind=kOutput, calls=%fused_computation.9 | convolution fusion | flops 17255366656 | bytes 69206016 | tf_op jit(solution)/shard_map/dot_general | solution.py:26
  362.6 0.0 copy-done
  362.6 40.1 %convert_bitcast_fusion = bf16[1024,8192]{0,1:T(8,128)(2,1)} fusion(bf16[1024,1024]{1,0:T(8,128)(2,1)S(1)} %copy-done, f32[8192,1024]{1,0:T(8,128)} %get-tuple-element.3, bf16[8192,1024]{1,0:T(8,128)(2,1)} %param.5), kind=kOutput, calls=%fused_computation.10 | convolution fusion | flops 17356029952 | bytes 69206016 | tf_op jit(solution)/shard_map/dot_general | solution.py:30
  402.7 0.0 reduce-scatter.2.cloned.1.call-update
  402.7 278.8 %reduce-scatter.2.cloned.1.call-done = bf16[256,8192]{0,1:T(8,128)(2,1)} async-done(((bf16[1024,8192]{0,1:T(8,128)(2,1)}), bf16[256,8192]{0,1:T(8,128)(2,1)}) %reduce-scatter.2.cloned.1.call-update) | async-done | bytes 4194320 | tf_op jit(solution)/shard_map/reduce_scatter | solution.py:29
Async XLA Ops:
  7.2 33.2 %all-gather.5.cloned.1.call-start = ((), (), s32[]{:S(2)}) async-start(), calls=%async_computation.2 | async-start | bytes 2359296 | tf_op jit(solution)/shard_map/all_gather | solution.py:24
  7.9 320.3 %all-gather.3.cloned.1.call-start = ((), (), s32[]{:S(2)}) async-start(), calls=%async_computation.1 | async-start | bytes 20971520 | tf_op jit(solution)/shard_map/all_gather | solution.py:25
  8.6 672.9 %reduce-scatter.2.cloned.1.call-start = ((), (), s32[]{:S(2)}) async-start(), calls=%async_computation.3 | async-start | bytes 20971520 | tf_op jit(solution)/shard_map/reduce_scatter | solution.py:29
  40.4 322.2 %copy-start = (bf16[1024,1024]{1,0:T(8,128)(2,1)S(1)}, bf16[1024,1024]{1,0:T(8,128)(2,1)}, u32[]{:S(2)}) copy-start(bf16[1024,1024]{1,0:T(8,128)(2,1)} %all-gather.5.cloned.1.call-done) | copy-start | bytes 6291460
Sparse Core Ops, SparseCore 0:
  9.9 30.4 all-gather.4
  41.9 286.2 all-gather.2
  402.9 278.6 reduce-scatter.1
where the time goes:
time: 688 us
  waiting for transfers between devices  600 us (87%)
  matrix products  74.5 us (11%)
  between operations  13.7 us (2%)
    all_gather x1, waiting for transfers between devices, per_device(): token_rows = lax.all_gather(tokens, 'col', axis=1, tiled=True)  288 us
    reduce_scatter x1, waiting for transfers between devices, per_device(): lax.psum_scatter(lax.dot_general(column_panel, pre_grad, (((1,), (1,)), (...  279 us
    dot_general x1, matrix products, per_device(): lax.dot_general(column_panel, pre_grad, (((1,), (1,)), ((), ())), preferr...  40.1 us
    dot_general x1, matrix products, per_device(): jnp.dot(token_rows, column_panel, preferred_element_type=jnp.float32)  34.3 us
    all_gather x1, waiting for transfers between devices, per_device(): column_panel = lax.all_gather(up_weight, 'row', axis=0, tiled=True)  31.7 us
  transfers between devices with their start and end apart: 3, of which 3 were waited for; matrix products, arithmetic and copies ran while one was open for 0% of the time, Pallas kernels for 0%

commit v1 on v0

--- a/solution.py
+++ b/solution.py
@@ -5,6 +5,19 @@
 
 gelu_c = 0.7978845608028654
 gelu_a = 0.044715
+
+
+def gather_around(x, axis, dim):
+    ways = lax.axis_size(axis)
+    up = [(d, (d + 1) % ways) for d in range(ways)]
+    down = [(d, (d - 1) % ways) for d in range(ways)]
+    earlier, later = ([x], [x])
+    for _ in range(ways // 2):
+        earlier.append(lax.ppermute(earlier[-1], axis, up))
+    for _ in range((ways - 1) // 2):
+        later.append(lax.ppermute(later[-1], axis, down))
+    line = jnp.concatenate([*earlier[::-1], *later[1:]], axis=dim)
+    return jnp.roll(line, (lax.axis_index(axis) - ways // 2) * x.shape[dim], axis=dim)
 
 
 def gelu_value(v):
@@ -22,7 +35,7 @@
 
 def per_device(tokens, up_weight, hidden_grad):
     column_panel = lax.all_gather(up_weight, "row", axis=0, tiled=True)
-    token_rows = lax.all_gather(tokens, "col", axis=1, tiled=True)
+    token_rows = gather_around(tokens, "col", 1)
     preact = jnp.dot(token_rows, column_panel, preferred_element_type=jnp.float32)
     hidden = gelu_value(preact).astype(jnp.bfloat16)
     pre_grad = (hidden_grad.astype(jnp.float32) * gelu_slope(preact)).astype(jnp.bfloat16)

time: 688 us -> 668 us (0.971)
  waiting for transfers between devices: 600 us -> 538 us
  local copies, waits for them, and re-layouts: 0.01 us -> 33.9 us
  starting transfers between devices: 0.11 us -> 7.01 us
    all_gather x1 -> x0, waiting for transfers between devices: 288 us -> none  [per_device(): token_rows = lax.all_gather(tokens, 'col', axis=1, tiled=True)]
    ppermute x0 -> x3, waiting for transfers between devices: none -> 257 us  [the longest x2 185 us: gather_around(): earlier.append(lax.ppermute(earlier[-1], axis, up))]
    all_gather x1, waiting for transfers between devices: 31.7 us -> 0.01 us  [per_device(): column_panel = lax.all_gather(up_weight, 'row', axis=0, tiled=True)]
    unnamed x2 -> x11, local copies, waits for them, and re-layouts: 0.01 us -> 29.4 us
    ppermute x0 -> x3, starting transfers between devices: none -> 6.93 us  [the longest x1 3.82 us: gather_around(): later.append(lax.ppermute(later[-1], axis, down))]
  transfers between devices with their start and end apart: 3 -> 5, of which waited for: 3 -> 4; matrix products, arithmetic and copies ran while one was open for 0% -> 5% of each run, Pallas kernels for 0% -> 0%
where the time goes in v1:
time: 668 us; the launch traced here: 667 us
  waiting for transfers between devices  538 us (81%)
  matrix products  74.7 us (11%)
  local copies, waits for them, and re-layouts  33.9 us (5%)
  between operations  14.1 us (2%)
  starting transfers between devices  7.01 us (1%)
    reduce_scatter x1, waiting for transfers between devices, per_device(): lax.psum_scatter(lax.dot_general(column_panel, pre_grad, (((1,), (1,)), (...  280 us
    ppermute x2, waiting for transfers between devices, gather_around(): earlier.append(lax.ppermute(earlier[-1], axis, up))  185 us
    ppermute x1, waiting for transfers between devices, gather_around(): later.append(lax.ppermute(later[-1], axis, down))  72.9 us
    dot_general x1, matrix products, per_device(): lax.dot_general(column_panel, pre_grad, (((1,), (1,)), ((), ())), preferr...  40.1 us
    dot_general x1, matrix products, per_device(): jnp.dot(token_rows, column_panel, preferred_element_type=jnp.float32)  34.5 us
    unnamed x11, local copies, waits for them, and re-layouts  29.4 us
  transfers between devices with their start and end apart: 5, of which 4 were waited for; matrix products, arithmetic and copies ran while one was open for 5% of the time, Pallas kernels for 0%

profile of v1, /device:TPU:0, one launch (start us, length us, event | category | flops | bytes accessed | tf_op | source)
XLA Modules:
  0.0 667.5 jit_solution(7844224912224045310)
XLA Ops:
  7.2 0.0 all-gather.2.cloned.1.call-start
  7.2 3.1 collective-permute-start
  10.3 92.9 %collective-permute-done = bf16[8192,256]{1,0:T(8,128)(2,1)} collective-permute-done((bf16[8192,256]{1,0:T(8,128)(2,1)}, bf16[8192,256]{1,0:T(8,128)(2,1)}, u32[]{:S(2)}, u32[]{:S(2)}) %collective-permute-start) | collective-permute-done | bytes 4194336 | tf_op jit(solution)/shard_map/ppermute | solution.py:16
  103.2 0.0 collective-permute-start.1
  103.2 3.8 collective-permute-start.2
  107.1 0.0 all-gather.2.cloned.1.call-update
  107.1 0.0 reduce-scatter.2.cloned.1.call-start
  107.2 0.0 copy-start
  107.2 91.6 %collective-permute-done.1 = bf16[8192,256]{1,0:T(8,128)(2,1)} collective-permute-done((bf16[8192,256]{1,0:T(8,128)(2,1)}, bf16[8192,256]{1,0:T(8,128)(2,1)}, u32[]{:S(2)}, u32[]{:S(2)}) %collective-permute-start.1) | collective-permute-done | bytes 4194336 | tf_op jit(solution)/shard_map/ppermute | solution.py:16
  198.8 4.5 constant_dynamic-update-slice_fusion.7
  203.3 4.5 constant_dynamic-update-slice_fusion.6
  207.8 4.5 constant_dynamic-update-slice_fusion.5
  212.3 72.9 %collective-permute-done.2 = bf16[8192,256]{1,0:T(8,128)(2,1)} collective-permute-done((bf16[8192,256]{1,0:T(8,128)(2,1)}, bf16[8192,256]{1,0:T(8,128)(2,1)}, u32[]{:S(2)}, u32[]{:S(2)}) %collective-permute-start.2) | collective-permute-done | bytes 4194336 | tf_op jit(solution)/shard_map/ppermute | solution.py:18
  285.2 4.5 constant_dynamic-update-slice_fusion.4
  289.7 4.5 constant_dynamic-update-slice_fusion.3
  294.2 4.5 constant_dynamic-update-slice_fusion.2
  298.7 0.0 copy-done
  298.7 2.4 constant_dynamic-update-slice_fusion.1
  301.1 4.5 constant_dynamic-update-slice_fusion
  305.6 0.0 all-gather.2.cloned.1.call-done
  305.6 0.0 copy-start.1
  305.6 34.5 %multiply_convert_fusion = (bf16[8192,1024]{1,0:T(8,128)(2,1)}, f32[8192,1024]{1,0:T(8,128)}) fusion(bf16[1024,1024]{1,0:T(8,128)(2,1)} %all-gather.2.cloned.1.call-done, bf16[8192,2048]{1,0:T(8,128)(2,1)} %constant_dynamic-update-slice_fusion, s32[]{:T(128)S(6)} %select_n.14), kind=kOutput, calls=%fused_computation.9 | convolution fusion | flops 17255366656 | bytes 69206016 | tf_op jit(solution)/shard_map/dot_general | solution.py:39
  340.1 0.0 copy-done.1
  340.1 40.1 %convert_bitcast_fusion = bf16[1024,8192]{0,1:T(8,128)(2,1)} fusion(bf16[1024,1024]{1,0:T(8,128)(2,1)S(1)} %copy-done.1, f32[8192,1024]{1,0:T(8,128)} %get-tuple-element.3, bf16[8192,1024]{1,0:T(8,128)(2,1)} %param.5), kind=kOutput, calls=%fused_computation.10 | convolution fusion | flops 17356029952 | bytes 69206016 | tf_op jit(solution)/shard_map/dot_general | solution.py:43
  380.2 0.0 reduce-scatter.2.cloned.1.call-update
  380.3 280.4 %reduce-scatter.2.cloned.1.call-done = bf16[256,8192]{0,1:T(8,128)(2,1)} async-done(((bf16[1024,8192]{0,1:T(8,128)(2,1)}), bf16[256,8192]{0,1:T(8,128)(2,1)}) %reduce-scatter.2.cloned.1.call-update) | async-done | bytes 4194320 | tf_op jit(solution)/shard_map/reduce_scatter | solution.py:42
Async XLA Ops:
  7.2 298.4 %all-gather.2.cloned.1.call-start = ((), (), s32[]{:S(2)}) async-start(), calls=%async_computation.1 | async-start | bytes 2359296 | tf_op jit(solution)/shard_map/all_gather | solution.py:37
  7.2 96.0 %collective-permute-start = (bf16[8192,256]{1,0:T(8,128)(2,1)}, bf16[8192,256]{1,0:T(8,128)(2,1)}, u32[]{:S(2)}, u32[]{:S(2)}) collective-permute-start(bf16[8192,256]{1,0:T(8,128)(2,1)} %param.3), channel_id=1, source_target_pairs={{0,1},{1,2},{2,3},{3,0},{4,5},{5,6},{6,7},{7,4},{8,9},{9,10},{10,1... | collective-permute-start | bytes 12582920 | tf_op jit(solution)/shard_map/ppermute | solution.py:16
  103.2 95.6 %collective-permute-start.1 = (bf16[8192,256]{1,0:T(8,128)(2,1)}, bf16[8192,256]{1,0:T(8,128)(2,1)}, u32[]{:S(2)}, u32[]{:S(2)}) collective-permute-start(bf16[8192,256]{1,0:T(8,128)(2,1)} %collective-permute-done), channel_id=1, source_target_pairs={{0,1},{1,2},{2,3},{3,0},{4,5},{5,6},{6,7},{7,4},{8,9},{9,10},{10,1... | collective-permute-start | bytes 12582920 | tf_op jit(solution)/shard_map/ppermute | solution.py:16
  103.2 181.9 %collective-permute-start.2 = (bf16[8192,256]{1,0:T(8,128)(2,1)}, bf16[8192,256]{1,0:T(8,128)(2,1)}, u32[]{:S(2)}, u32[]{:S(2)}) collective-permute-start(bf16[8192,256]{1,0:T(8,128)(2,1)} %param.3), channel_id=1, source_target_pairs={{0,3},{1,0},{2,1},{3,2},{4,7},{5,4},{6,5},{7,6},{8,11},{9,8},{10,9... | collective-permute-start | bytes 12582920 | tf_op jit(solution)/shard_map/ppermute | solution.py:18
  107.1 553.6 %reduce-scatter.2.cloned.1.call-start = ((), (), s32[]{:S(2)}) async-start(), calls=%async_computation.2 | async-start | bytes 20971520 | tf_op jit(solution)/shard_map/reduce_scatter | solution.py:42
  107.2 191.6 %copy-start = (bf16[8192,256]{1,0:T(8,128)(2,1)S(1)}, bf16[8192,256]{1,0:T(8,128)(2,1)}, u32[]{:S(2)}) copy-start(bf16[8192,256]{1,0:T(8,128)(2,1)} %param.3) | copy-start | bytes 12582916
  305.6 34.5 %copy-start.1 = (bf16[1024,1024]{1,0:T(8,128)(2,1)S(1)}, bf16[1024,1024]{1,0:T(8,128)(2,1)}, u32[]{:S(2)}) copy-start(bf16[1024,1024]{1,0:T(8,128)(2,1)} %all-gather.2.cloned.1.call-done) | copy-start | bytes 6291460
Sparse Core Ops, SparseCore 0:
  107.2 25.9 all-gather.1
  380.4 280.2 reduce-scatter.1
